TPU v7x, 32 devices: a whole 2x2x4 slice. The times are simulated.
32 devices in a mesh: groups: 2 (over y), seq: 4 (over z), rep: 2 (over x), fsdp: 2 (over core).
Axes of the slice: x: 2, y: 2, z: 4, core: 2. Of those that a mesh axis runs over, the one named last changes fastest.
Arguments:
- activations: bfloat16 [8, 512, 2048], P(('groups', 'rep', 'fsdp'), 'seq'), parts along dimension 0, may hold values from -6 to 6
- queries: bfloat16 [8, 512, 2048], P(('groups', 'rep', 'fsdp'), 'seq'), parts along dimension 0, may hold values from -102 to 102
- key_weight: bfloat16 [2048, 512], P(('seq', 'fsdp')), may hold values from -0.125 to 0.125
- value_weight: bfloat16 [2048, 512], P(('seq', 'fsdp')), may hold values from -0.125 to 0.125
- segment_ids: int32 [8, 512], P(('groups', 'rep', 'fsdp'), 'seq'), parts along dimension 0, may hold values from 0 to 3, never falling along the last dimension, each value on 1 to 384 neighbouring positions
- out_grad: bfloat16 [8, 512, 2048], P(('groups', 'rep', 'fsdp'), 'seq'), parts along dimension 0, may hold values from -6 to 6
Outputs:
- context: bfloat16 [8, 512, 2048], P(('groups', 'rep', 'fsdp'), 'seq'), parts along dimension 0
- query_grad: bfloat16 [8, 512, 2048], P(('groups', 'rep', 'fsdp'), 'seq'), parts along dimension 0
- input_grad: bfloat16 [8, 512, 2048], P(('groups', 'rep', 'fsdp'), 'seq'), parts along dimension 0
- key_weight_grad: bfloat16 [4096, 512], P(('groups', 'seq', 'fsdp')), parts along dimension 0
- value_weight_grad: bfloat16 [4096, 512], P(('groups', 'seq', 'fsdp')), parts along dimension 0
There are 2 independent parts, one for each index of `groups`. A program takes and returns all parts, laid end to end along the dimension named above; an argument that names none is the same for every part. Nothing has to cross between parts.
Inputs may be any that keep to these rules, and one draw needn't show every extreme that they name: `segment_ids`: document numbers never fall along a sequence; a document covers at most 384 positions.
All inputs are finite; a program needn't handle non-finite values.
Results may differ from a plain program's by a relative error of at most 0.025.
The roundings to bfloat16 on the way count: a program that leaves them out, or rounds other values in their place, can miss the bound.
Values may be sent and summed in bfloat16 or wider, within the bound.
No kernel may reach another device: no remote copies, remote signals or barrier semaphores. Data moves between devices by JAX's collectives and lax.ppermute only.
A program may use at most 64 MiB of HBM per device.

v0:
```python
import math
import jax
import jax.numpy as jnp
from jax import lax
from jax.sharding import PartitionSpec as P

HEADS = 16
KV_HEADS = 4
HEAD_DIM = 128
masked_low = -1e30


def block_mask(seg_all, row_start, col_start, block_width):
    row_pos = row_start + lax.iota(jnp.int32, block_width)
    col_pos = col_start + lax.iota(jnp.int32, block_width)
    seg_rows = lax.dynamic_slice_in_dim(seg_all, row_start, block_width)
    seg_cols = lax.dynamic_slice_in_dim(seg_all, col_start, block_width)
    return (col_pos[None, :] <= row_pos[:, None]) & (seg_cols[None, :] == seg_rows[:, None])


def block_scores(query_block, key_block, inv_root):
    return (
        jnp.einsum("qhd,khd->hqk", query_block, key_block, preferred_element_type=jnp.float32)
        * inv_root
    )


def take_block(source, index, block_width):
    return lax.dynamic_slice_in_dim(source, index * block_width, block_width, 0)


def attend(query_part, key_part, value_part, seg_all):
    length, heads_here, head_size = query_part.shape
    block_width = min(512, length)
    block_count = length // block_width
    inv_root = 1.0 / math.sqrt(head_size)

    def stats_row(i, log_totals):
        query_block = take_block(query_part, i, block_width)

        def stats_inner(j, state_now):
            running_max, running_sum = state_now
            scores = block_scores(query_block, take_block(key_part, j, block_width), inv_root)
            allowed = block_mask(seg_all, i * block_width, j * block_width, block_width)[None]
            scores = jnp.where(allowed, scores, masked_low)
            new_max = jnp.maximum(running_max, jnp.max(scores, axis=-1))
            weights = jnp.where(allowed, jnp.exp(scores - new_max[..., None]), 0.0)
            running_sum = running_sum * jnp.exp(running_max - new_max) + jnp.sum(weights, axis=-1)
            return (new_max, running_sum)

        start_state = (
            jnp.full((heads_here, block_width), masked_low, jnp.float32),
            jnp.zeros((heads_here, block_width), jnp.float32),
        )
        running_max, running_sum = lax.fori_loop(0, i + 1, stats_inner, start_state)
        return lax.dynamic_update_slice_in_dim(
            log_totals, running_max + jnp.log(running_sum), i * block_width, 1
        )

    log_totals = lax.fori_loop(
        0, block_count, stats_row, jnp.zeros((heads_here, length), jnp.float32)
    )

    def out_row(i, out_all):
        query_block = take_block(query_part, i, block_width)
        log_block = lax.dynamic_slice_in_dim(log_totals, i * block_width, block_width, 1)

        def out_inner(j, accum_out):
            scores = block_scores(query_block, take_block(key_part, j, block_width), inv_root)
            allowed = block_mask(seg_all, i * block_width, j * block_width, block_width)[None]
            probs_low = jnp.where(allowed, jnp.exp(scores - log_block[..., None]), 0.0).astype(
                jnp.bfloat16
            )
            return accum_out + jnp.einsum(
                "hqk,khd->qhd",
                probs_low,
                take_block(value_part, j, block_width),
                preferred_element_type=jnp.float32,
            )

        accum_out = lax.fori_loop(
            0, i + 1, out_inner, jnp.zeros((block_width, heads_here, head_size), jnp.float32)
        )
        return lax.dynamic_update_slice_in_dim(
            out_all, accum_out.astype(jnp.bfloat16), i * block_width, 0
        )

    out_all = lax.fori_loop(
        0, block_count, out_row, jnp.zeros((length, heads_here, head_size), jnp.bfloat16)
    )
    return (out_all, log_totals)


def attend_grads(query_part, key_part, value_part, seg_all, out_part, log_totals, grad_part):
    length, heads_here, head_size = query_part.shape
    block_width = min(512, length)
    block_count = length // block_width
    inv_root = 1.0 / math.sqrt(head_size)
    row_dots = jnp.einsum("qhd,qhd->hq", grad_part, out_part, preferred_element_type=jnp.float32)

    def grad_row(i, state_now):
        query_all, key_all, value_all = state_now
        query_block = take_block(query_part, i, block_width)
        grad_block = take_block(grad_part, i, block_width)
        log_block = lax.dynamic_slice_in_dim(log_totals, i * block_width, block_width, 1)
        dots_block = lax.dynamic_slice_in_dim(row_dots, i * block_width, block_width, 1)

        def grad_inner(j, inner_state):
            query_accum, key_accum, value_accum = inner_state
            key_block = take_block(key_part, j, block_width)
            value_block = take_block(value_part, j, block_width)
            scores = block_scores(query_block, key_block, inv_root)
            allowed = block_mask(seg_all, i * block_width, j * block_width, block_width)[None]
            probs = jnp.where(allowed, jnp.exp(scores - log_block[..., None]), 0.0)
            probs_low = probs.astype(jnp.bfloat16)
            value_new = take_block(value_accum, j, block_width) + jnp.einsum(
                "hqk,qhd->khd", probs_low, grad_block, preferred_element_type=jnp.float32
            )
            value_accum = lax.dynamic_update_slice_in_dim(
                value_accum, value_new, j * block_width, 0
            )
            prob_grad = jnp.einsum(
                "qhd,khd->hqk", grad_block, value_block, preferred_element_type=jnp.float32
            )
            score_grad = (probs * (prob_grad - dots_block[..., None])).astype(jnp.bfloat16)
            query_accum = query_accum + jnp.einsum(
                "hqk,khd->qhd", score_grad, key_block, preferred_element_type=jnp.float32
            )
            key_new = take_block(key_accum, j, block_width) + jnp.einsum(
                "hqk,qhd->khd", score_grad, query_block, preferred_element_type=jnp.float32
            )
            key_accum = lax.dynamic_update_slice_in_dim(key_accum, key_new, j * block_width, 0)
            return (query_accum, key_accum, value_accum)

        start_state = (
            jnp.zeros((block_width, heads_here, head_size), jnp.float32),
            key_all,
            value_all,
        )
        query_accum, key_all, value_all = lax.fori_loop(0, i + 1, grad_inner, start_state)
        query_all = lax.dynamic_update_slice_in_dim(
            query_all, (query_accum * inv_root).astype(jnp.bfloat16), i * block_width, 0
        )
        return (query_all, key_all, value_all)

    zero_grads = jnp.zeros((length, heads_here, head_size), jnp.float32)
    start_all = (jnp.zeros((length, heads_here, head_size), jnp.bfloat16), zero_grads, zero_grads)
    query_all, key_all, value_all = lax.fori_loop(0, block_count, grad_row, start_all)
    return (query_all, (key_all * inv_root).astype(jnp.bfloat16), value_all.astype(jnp.bfloat16))


def body(activations, queries, key_weight, value_weight, segment_ids, out_grad):
    rows_here = activations.shape[1]
    inputs = activations[0]
    kv_width = key_weight.shape[1]
    seq_devices = lax.axis_size("seq")
    heads_here = HEADS // seq_devices
    kv_group = HEADS // KV_HEADS
    stacked = jnp.concatenate([key_weight, value_weight], axis=1)
    columns = inputs
    projected = jnp.dot(
        columns,
        lax.all_gather(stacked, ("seq", "fsdp"), axis=0, tiled=True),
        preferred_element_type=jnp.float32,
    )
    projected = projected.astype(jnp.bfloat16)
    key_rows = projected[:, :kv_width].reshape(rows_here, KV_HEADS, HEAD_DIM)
    value_rows = projected[:, kv_width:].reshape(rows_here, KV_HEADS, HEAD_DIM)
    kv_copies = max(kv_group // heads_here, 1)
    query_heads = queries[0].reshape(rows_here, HEADS, HEAD_DIM)
    sent = (
        query_heads,
        jnp.repeat(key_rows, kv_copies, axis=1),
        jnp.repeat(value_rows, kv_copies, axis=1),
    )
    query_part, key_part, value_part = (
        lax.all_to_all(sent[0], "seq", split_axis=1, concat_axis=0, tiled=True),
        lax.all_to_all(sent[1], "seq", split_axis=1, concat_axis=0, tiled=True),
        lax.all_to_all(sent[2], "seq", split_axis=1, concat_axis=0, tiled=True),
    )
    widen_by = heads_here // key_part.shape[1]
    key_part = jnp.repeat(key_part, widen_by, axis=1)
    value_part = jnp.repeat(value_part, widen_by, axis=1)
    seg_all = lax.all_gather(segment_ids[0], "seq", axis=0, tiled=True)
    out_part, log_totals = attend(query_part, key_part, value_part, seg_all)
    context = lax.all_to_all(out_part, "seq", split_axis=0, concat_axis=1, tiled=True).reshape(
        1, rows_here, HEADS * HEAD_DIM
    )
    grad_part = lax.all_to_all(
        out_grad[0].reshape(rows_here, HEADS, HEAD_DIM),
        "seq",
        split_axis=1,
        concat_axis=0,
        tiled=True,
    )
    query_back, key_back, value_back = attend_grads(
        query_part, key_part, value_part, seg_all, out_part, log_totals, grad_part
    )
    query_tok, key_tok, value_tok = (
        lax.all_to_all(query_back, "seq", split_axis=0, concat_axis=1, tiled=True),
        lax.all_to_all(key_back, "seq", split_axis=0, concat_axis=1, tiled=True),
        lax.all_to_all(value_back, "seq", split_axis=0, concat_axis=1, tiled=True),
    )
    key_sum = (
        key_tok.reshape(rows_here, KV_HEADS, kv_group, HEAD_DIM).astype(jnp.float32).sum(axis=2)
    )
    value_sum = (
        value_tok.reshape(rows_here, KV_HEADS, kv_group, HEAD_DIM).astype(jnp.float32).sum(axis=2)
    )
    grad_kv = jnp.concatenate(
        [
            key_sum.astype(jnp.bfloat16).reshape(rows_here, kv_width),
            value_sum.astype(jnp.bfloat16).reshape(rows_here, kv_width),
        ],
        axis=1,
    )
    input_grad = lax.dot_general(
        grad_kv,
        lax.all_gather(stacked, ("seq", "fsdp"), axis=0, tiled=True),
        (((1,), (1,)), ((), ())),
        preferred_element_type=jnp.float32,
    )
    input_grad = input_grad.astype(jnp.bfloat16).reshape(1, rows_here, inputs.shape[1])
    columns = inputs
    grad_shard = lax.psum_scatter(
        lax.dot_general(
            columns, grad_kv, (((0,), (0,)), ((), ())), preferred_element_type=jnp.float32
        ).astype(jnp.bfloat16),
        ("seq", "fsdp"),
        scatter_dimension=0,
        tiled=True,
    ).astype(jnp.float32)
    grad_total = lax.psum(grad_shard, "rep").astype(jnp.bfloat16)
    query_grad = query_tok.reshape(1, rows_here, HEADS * HEAD_DIM)
    return (context, query_grad, input_grad, grad_total[:, :kv_width], grad_total[:, kv_width:])


def solution(mesh):
    return jax.shard_map(
        body,
        mesh=mesh,
        in_specs=(
            P(("groups", "rep", "fsdp"), "seq", None),
            P(("groups", "rep", "fsdp"), "seq", None),
            P(("seq", "fsdp"), None),
            P(("seq", "fsdp"), None),
            P(("groups", "rep", "fsdp"), "seq"),
            P(("groups", "rep", "fsdp"), "seq", None),
        ),
        out_specs=(
            P(("groups", "rep", "fsdp"), "seq", None),
            P(("groups", "rep", "fsdp"), "seq", None),
            P(("groups", "rep", "fsdp"), "seq", None),
            P(("groups", "seq", "fsdp"), None),
            P(("groups", "seq", "fsdp"), None),
        ),
        check_vma=False,
    )
```

profile of v0, /device:TPU:0, one launch (start us, length us, event | category | flops | bytes accessed | tf_op | source)
XLA Modules:
  0.0 248.5 jit_solution(1533762481953320926)
XLA Ops:
  7.2 1.9 pad_maximum_fusion
  9.2 2.0 copy.45
  11.2 6.3 %all-to-all-start.1 = ((bf16[128,16,128]{0,2,1:T(8,128)(2,1)}), bf16[128,16,128]{0,2,1:T(8,128)(2,1)S(1)}, u32[]{:S(2)}, u32[]{:S(2)}) async-start(bf16[128,16,128]{0,2,1:T(8,128)(2,1)} %bitcast.9), calls=%async_computation.1 | async-start | bytes 1048576 | tf_op jit(solution)/shard_map/all_to_all | solution.py:177
  17.5 2.0 copy.52
  19.6 24.7 %all-to-all-done.1 = bf16[128,16,128]{0,2,1:T(8,128)(2,1)S(1)} async-done(((bf16[128,16,128]{0,2,1:T(8,128)(2,1)}), bf16[128,16,128]{0,2,1:T(8,128)(2,1)S(1)}, u32[]{:S(2)}, u32[]{:S(2)}) %all-to-all-start.1) | async-done | bytes 524320 | tf_op jit(solution)/shard_map/all_to_all | solution.py:177
  44.2 3.6 %all-to-all-start.4 = ((bf16[128,16,128]{0,2,1:T(8,128)(2,1)}), bf16[128,16,128]{0,2,1:T(8,128)(2,1)S(1)}, u32[]{:S(2)}, u32[]{:S(2)}) async-start(bf16[128,16,128]{0,2,1:T(8,128)(2,1)} %bitcast.22), calls=%async_computation.4 | async-start | bytes 1048576 | tf_op jit(solution)/shard_map/all_to_all | solution.py:189
  47.9 21.7 %all-gather = s32[1,512]{1,0:T(1,128)S(1)} all-gather(s32[1,128]{1,0:T(1,128)S(1)} %copy-done.3), channel_id=2, replica_groups=mesh['groups'=2,'seq'=4,'rep'=2,'fsdp'=2] {'seq'}, dimensions={1}, use_global_device_ids=true | all-gather | bytes 2560 | tf_op jit(solution)/shard_map/all_gather | solution.py:184
  69.5 9.1 %all-gather.3.cloned.1.call-done = bf16[2048,1024]{1,0:T(8,128)(2,1)} async-done(((bf16[256,1024]{1,0:T(8,128)(2,1)}), bf16[2048,1024]{1,0:T(8,128)(2,1)}) %all-gather.3.cloned.1.call-update) | async-done | bytes 4194320 | tf_op jit(solution)/shard_map/all_gather | solution.py:163
  78.7 3.5 %fusion.11 = bf16[128,1024]{0,1:T(8,128)(2,1)S(1)} fusion(bf16[2048,1024]{1,0:T(8,128)(2,1)} %all-gather.3.cloned.1.call-done, bf16[1,128,2048]{2,1,0:T(8,128)(2,1)S(1)} %copy-done), kind=kOutput, calls=%fused_computation.22 | convolution fusion | flops 537001984 | bytes 4980736 | tf_op jit(solution)/shard_map/dot_general | solution.py:161
  82.2 0.8 copy.44
  83.0 3.3 %all-to-all-start = ((bf16[128,4,128]{2,0,1:T(8,128)(2,1)}), bf16[128,4,128]{2,0,1:T(8,128)(2,1)S(1)}, u32[]{:S(2)}, u32[]{:S(2)}) async-start(bf16[128,4,128]{2,0,1:T(8,128)(2,1)} %copy.44), calls=%async_computation | async-start | bytes 262144 | tf_op jit(solution)/shard_map/all_to_all | solution.py:178
  86.5 0.3 copy.47
  86.8 0.3 copy.54
  87.1 0.8 copy.48
  87.9 4.8 %all-to-all-done = bf16[128,4,128]{2,0,1:T(8,128)(2,1)S(1)} async-done(((bf16[128,4,128]{2,0,1:T(8,128)(2,1)}), bf16[128,4,128]{2,0,1:T(8,128)(2,1)S(1)}, u32[]{:S(2)}, u32[]{:S(2)}) %all-to-all-start) | async-done | bytes 131104 | tf_op jit(solution)/shard_map/all_to_all | solution.py:178
  92.7 3.3 %all-to-all-start.2 = ((bf16[128,4,128]{2,0,1:T(8,128)(2,1)}), bf16[128,4,128]{2,0,1:T(8,128)(2,1)S(1)}, u32[]{:S(2)}, u32[]{:S(2)}) async-start(bf16[128,4,128]{2,0,1:T(8,128)(2,1)} %copy.48), calls=%async_computation.2 | async-start | bytes 262144 | tf_op jit(solution)/shard_map/all_to_all | solution.py:179
  96.0 0.9 fusion.3
  96.9 1.0 select_reduce_fusion
  98.0 0.9 fusion.10
  99.0 1.2 copy.60
  100.2 1.8 all-to-all-done.2
  101.9 3.5 %all-to-all-start.7 = ((bf16[512,4,128]{2,1,0:T(4,128)(2,1)}), bf16[512,4,128]{2,1,0:T(4,128)(2,1)S(1)}, u32[]{:S(2)}, u32[]{:S(2)}) async-start(bf16[512,4,128]{2,1,0:T(4,128)(2,1)} %copy.60), calls=%async_computation.7 | async-start | bytes 1048576 | tf_op jit(solution)/shard_map/all_to_all | solution.py:202
  105.4 3.9 %fusion.12 = (f32[4,512]{1,0:T(4,128)S(1)}, bf16[4,512,128]{2,1,0:T(8,128)(2,1)S(1)}) fusion(bf16[4,128,4,128]{3,1,0,2:T(8,128)(2,1)S(1)} %copy.54, bf16[512,128]{1,0:T(8,128)(2,1)S(1)} %bitcast.111, f32[4,512,512]{2,1,0:T(8,128)} %copy-done.1, f32[4,512]{1,0:T(4,128)S(1)} %log_add_fusion, pred[512,512]{0,1:T(8,128)(4,1)S(1)} %fusion.13), kind=kOutput, calls=%fused_computation.24 | convolution fusion | flops 273938432 | bytes 5652480 | tf_op jit(solution)/shard_map/while/body/eval_jaxpr/while/body/hqk,khd->qhd/dot_general | solution.py:74
  109.3 1.4 fusion
  110.8 0.7 fusion.8
  111.5 0.6 copy-done.4
  112.1 1.2 copy.58
  113.3 5.2 %all-to-all-done.7 = bf16[512,4,128]{2,1,0:T(4,128)(2,1)S(1)} async-done(((bf16[512,4,128]{2,1,0:T(4,128)(2,1)}), bf16[512,4,128]{2,1,0:T(4,128)(2,1)S(1)}, u32[]{:S(2)}, u32[]{:S(2)}) %all-to-all-start.7) | async-done | bytes 524320 | tf_op jit(solution)/shard_map/all_to_all | solution.py:202
  118.5 3.5 %all-to-all-start.6 = ((bf16[512,4,128]{2,1,0:T(4,128)(2,1)}), bf16[512,4,128]{2,1,0:T(4,128)(2,1)S(1)}, u32[]{:S(2)}, u32[]{:S(2)}) async-start(bf16[512,4,128]{2,1,0:T(4,128)(2,1)} %copy.58), calls=%async_computation.6 | async-start | bytes 1048576 | tf_op jit(solution)/shard_map/all_to_all | solution.py:201
  122.0 0.2 reduce-scatter.2.cloned.1.call-start
  122.2 0.7 reduce_sum.48
  123.0 12.3 %all-to-all-done.6 = bf16[512,4,128]{2,1,0:T(4,128)(2,1)S(1)} async-done(((bf16[512,4,128]{2,1,0:T(4,128)(2,1)}), bf16[512,4,128]{2,1,0:T(4,128)(2,1)S(1)}, u32[]{:S(2)}, u32[]{:S(2)}) %all-to-all-start.6) | async-done | bytes 524320 | tf_op jit(solution)/shard_map/all_to_all | solution.py:201
  135.3 0.7 reduce_sum.45
  136.1 3.2 %convert_bitcast_fusion = bf16[2048,1024]{0,1:T(8,128)(2,1)} fusion(bf16[1,128,2048]{2,1,0:T(8,128)(2,1)S(1)} %copy-done, bf16[128,512]{0,1:T(8,128)(2,1)S(1)} %bitcast.98, bf16[128,512]{0,1:T(8,128)(2,1)S(1)} %bitcast.100), kind=kOutput, calls=%fused_computation.6 | convolution fusion | flops 539492352 | bytes 4980736 | tf_op jit(solution)/shard_map/dot_general | solution.py:226
  139.4 1.2 copy.50
  140.6 3.5 %all-to-all-start.3 = ((bf16[512,4,128]{2,1,0:T(4,128)(2,1)}), bf16[512,4,128]{2,1,0:T(4,128)(2,1)S(1)}, u32[]{:S(2)}, u32[]{:S(2)}) async-start(bf16[512,4,128]{2,1,0:T(4,128)(2,1)} %copy.50), calls=%async_computation.3 | async-start | bytes 1048576 | tf_op jit(solution)/shard_map/all_to_all | solution.py:186
  144.1 0.9 fusion.9
  145.0 1.2 copy.56
  146.2 19.1 %all-to-all-done.3 = bf16[512,4,128]{2,1,0:T(4,128)(2,1)S(1)} async-done(((bf16[512,4,128]{2,1,0:T(4,128)(2,1)}), bf16[512,4,128]{2,1,0:T(4,128)(2,1)S(1)}, u32[]{:S(2)}, u32[]{:S(2)}) %all-to-all-start.3) | async-done | bytes 524320 | tf_op jit(solution)/shard_map/all_to_all | solution.py:186
  165.3 4.3 %all-to-all-start.5 = ((bf16[512,4,128]{2,1,0:T(4,128)(2,1)}), bf16[512,4,128]{2,1,0:T(4,128)(2,1)S(1)}, u32[]{:S(2)}, u32[]{:S(2)}) async-start(bf16[512,4,128]{2,1,0:T(4,128)(2,1)} %copy.56), calls=%async_computation.5 | async-start | bytes 1048576 | tf_op jit(solution)/shard_map/all_to_all | solution.py:200
  169.6 34.6 %reduce-scatter.2.cloned.1.call-done = bf16[256,1024]{0,1:T(8,128)(2,1)} async-done(((bf16[2048,1024]{0,1:T(8,128)(2,1)}), bf16[256,1024]{0,1:T(8,128)(2,1)}) %reduce-scatter.2.cloned.1.call-update) | async-done | bytes 524304 | tf_op jit(solution)/shard_map/reduce_scatter | solution.py:225
  204.4 1.2 reshape.232
  205.8 1.2 reshape.233
  207.0 4.5 %fusion.5 = bf16[1,128,2048]{2,1,0:T(8,128)(2,1)} fusion(bf16[2048,1024]{1,0:T(8,128)(2,1)} %all-gather.3.cloned.1.call-done, bf16[128,512]{0,1:T(8,128)(2,1)S(1)} %bitcast.99, bf16[128,512]{0,1:T(8,128)(2,1)S(1)} %bitcast.101), kind=kOutput, calls=%fused_computation.11 | convolution fusion | flops 537657344 | bytes 4980736 | tf_op jit(solution)/shard_map/dot_general | solution.py:217
  211.5 27.7 %all-reduce.2.cloned.1.call-done = bf16[256,1024]{0,1:T(8,128)(2,1)} async-done(((bf16[256,1024]{0,1:T(8,128)(2,1)}), bf16[256,1024]{0,1:T(8,128)(2,1)}) %all-reduce.2.cloned.1.call-update) | async-done | bytes 524304 | tf_op jit(solution)/shard_map/psum | solution.py:233
  239.2 1.1 fusion.25
  240.2 0.8 copy.63
  241.1 0.8 copy.62
  (26 shorter events, 1.0 us)
Async XLA Ops:
  7.2 71.5 %copy-start = (bf16[1,128,2048]{2,1,0:T(8,128)(2,1)S(1)}, bf16[1,128,2048]{2,1,0:T(8,128)(2,1)}, u32[]{:S(2)}) copy-start(bf16[1,128,2048]{2,1,0:T(8,128)(2,1)} %param.6) | copy-start | bytes 1572868
  7.2 40.7 %copy-start.3 = (s32[1,128]{1,0:T(1,128)S(1)}, s32[1,128]{1,0:T(1,128)}, u32[]{:S(2)}) copy-start(s32[1,128]{1,0:T(1,128)} %param.10) | copy-start | bytes 1540
  7.2 71.5 %all-gather.3.cloned.1.call-start = ((), (), s32[]{:S(2)}) async-start(), calls=%async_computation.9 | async-start | bytes 4718592 | tf_op jit(solution)/shard_map/all_gather | solution.py:163
  11.2 33.0 %all-to-all-start.1 = ((bf16[128,16,128]{0,2,1:T(8,128)(2,1)}), bf16[128,16,128]{0,2,1:T(8,128)(2,1)S(1)}, u32[]{:S(2)}, u32[]{:S(2)}) async-start(bf16[128,16,128]{0,2,1:T(8,128)(2,1)} %bitcast.9), calls=%async_computation.1 | async-start | bytes 1048576 | tf_op jit(solution)/shard_map/all_to_all | solution.py:177
  44.2 38.7 %all-to-all-start.4 = ((bf16[128,16,128]{0,2,1:T(8,128)(2,1)}), bf16[128,16,128]{0,2,1:T(8,128)(2,1)S(1)}, u32[]{:S(2)}, u32[]{:S(2)}) async-start(bf16[128,16,128]{0,2,1:T(8,128)(2,1)} %bitcast.22), calls=%async_computation.4 | async-start | bytes 1048576 | tf_op jit(solution)/shard_map/all_to_all | solution.py:189
  83.0 9.7 %all-to-all-start = ((bf16[128,4,128]{2,0,1:T(8,128)(2,1)}), bf16[128,4,128]{2,0,1:T(8,128)(2,1)S(1)}, u32[]{:S(2)}, u32[]{:S(2)}) async-start(bf16[128,4,128]{2,0,1:T(8,128)(2,1)} %copy.44), calls=%async_computation | async-start | bytes 262144 | tf_op jit(solution)/shard_map/all_to_all | solution.py:178
  92.7 9.2 %all-to-all-start.2 = ((bf16[128,4,128]{2,0,1:T(8,128)(2,1)}), bf16[128,4,128]{2,0,1:T(8,128)(2,1)S(1)}, u32[]{:S(2)}, u32[]{:S(2)}) async-start(bf16[128,4,128]{2,0,1:T(8,128)(2,1)} %copy.48), calls=%async_computation.2 | async-start | bytes 262144 | tf_op jit(solution)/shard_map/all_to_all | solution.py:179
  96.9 2.0 copy-start.1
  101.9 16.6 %all-to-all-start.7 = ((bf16[512,4,128]{2,1,0:T(4,128)(2,1)}), bf16[512,4,128]{2,1,0:T(4,128)(2,1)S(1)}, u32[]{:S(2)}, u32[]{:S(2)}) async-start(bf16[512,4,128]{2,1,0:T(4,128)(2,1)} %copy.60), calls=%async_computation.7 | async-start | bytes 1048576 | tf_op jit(solution)/shard_map/all_to_all | solution.py:202
  105.4 3.9 %copy-start.2 = (f32[4,512,512]{2,1,0:T(8,128)S(1)}, f32[4,512,512]{2,1,0:T(8,128)}, u32[]{:S(2)}) copy-start(f32[4,512,512]{2,1,0:T(8,128)} %copy-done.1) | copy-start | bytes 12582916
  110.7 1.4 copy-start.4
  118.5 16.8 %all-to-all-start.6 = ((bf16[512,4,128]{2,1,0:T(4,128)(2,1)}), bf16[512,4,128]{2,1,0:T(4,128)(2,1)S(1)}, u32[]{:S(2)}, u32[]{:S(2)}) async-start(bf16[512,4,128]{2,1,0:T(4,128)(2,1)} %copy.58), calls=%async_computation.6 | async-start | bytes 1048576 | tf_op jit(solution)/shard_map/all_to_all | solution.py:201
  122.0 82.2 %reduce-scatter.2.cloned.1.call-start = ((), (), s32[]{:S(2)}) async-start(), calls=%async_computation.10 | async-start | bytes 4718592 | tf_op jit(solution)/shard_map/reduce_scatter | solution.py:225
  139.3 4.7 %copy-start.5 = (bf16[4,512,512]{1,2,0:T(8,128)(2,1)S(1)}, bf16[4,512,512]{1,2,0:T(8,128)(2,1)}, u32[]{:S(2)}) copy-start(bf16[4,512,512]{1,2,0:T(8,128)(2,1)} %copy-done.4) | copy-start | bytes 6291460
  140.6 24.7 %all-to-all-start.3 = ((bf16[512,4,128]{2,1,0:T(4,128)(2,1)}), bf16[512,4,128]{2,1,0:T(4,128)(2,1)S(1)}, u32[]{:S(2)}, u32[]{:S(2)}) async-start(bf16[512,4,128]{2,1,0:T(4,128)(2,1)} %copy.50), calls=%async_computation.3 | async-start | bytes 1048576 | tf_op jit(solution)/shard_map/all_to_all | solution.py:186
  165.3 40.3 %all-to-all-start.5 = ((bf16[512,4,128]{2,1,0:T(4,128)(2,1)}), bf16[512,4,128]{2,1,0:T(4,128)(2,1)S(1)}, u32[]{:S(2)}, u32[]{:S(2)}) async-start(bf16[512,4,128]{2,1,0:T(4,128)(2,1)} %copy.56), calls=%async_computation.5 | async-start | bytes 1048576 | tf_op jit(solution)/shard_map/all_to_all | solution.py:200
  169.6 69.6 %all-reduce.2.cloned.1.call-start = ((), (), s32[]{:S(2)}) async-start(), calls=%async_computation.11 | async-start | bytes 1048576 | tf_op jit(solution)/shard_map/psum | solution.py:233
Sparse Core Ops, SparseCore 0:
  10.2 68.4 all-gather.2
  139.5 64.6 reduce-scatter.1
  206.5 32.6 all-reduce.1
where the time goes:
time: 249 us; the launch traced here: 248 us
  waiting for transfers between devices  139 us (56%)
  starting transfers between devices  31.6 us (13%)
  blocking collectives  21.7 us (9%)
  matrix products  19.9 us (8%)
  local copies, waits for them, and re-layouts  17.4 us (7%)
  between operations  14 us (6%)
  other arithmetic  4.52 us (2%)
    reduce_scatter x1, waiting for transfers between devices, body(): lax.psum_scatter(lax.dot_general(columns, grad_kv, (((0,), (0,)), ((), ()...  34.6 us
    psum x1, waiting for transfers between devices, body(): grad_total = lax.psum(grad_shard, 'rep').astype(jnp.bfloat16)  27.7 us
    all_to_all x1, waiting for transfers between devices, body(): lax.all_to_all(sent[0], 'seq', split_axis=1, concat_axis=0, tiled=True)  24.7 us
    all_gather x1, blocking collectives, body(): seg_all = lax.all_gather(segment_ids[0], 'seq', axis=0, tiled=True)  21.7 us
    all_to_all x1, waiting for transfers between devices, body(): lax.all_to_all(out_part, 'seq', split_axis=0, concat_axis=1, tiled=True)  19.1 us
    all_to_all x1, waiting for transfers between devices, body(): lax.all_to_all(key_back, 'seq', split_axis=0, concat_axis=1, tiled=True)  12.3 us
    all_gather x1, waiting for transfers between devices, body(): lax.all_gather(stacked, ('seq', 'fsdp'), axis=0, tiled=True)  9.14 us
    unnamed x16, local copies, waits for them, and re-layouts  6.44 us
  transfers between devices with their start and end apart: 11, of which 9 were waited for; matrix products, arithmetic and copies ran while one was open for 13% of the time, Pallas kernels for 0%

commit v1 on v0

--- a/solution.py
+++ b/solution.py
@@ -230,7 +230,7 @@
         scatter_dimension=0,
         tiled=True,
     ).astype(jnp.float32)
-    grad_total = lax.psum(grad_shard, "rep").astype(jnp.bfloat16)
+    grad_total = jnp.sum(lax.all_gather(grad_shard, "rep"), axis=0).astype(jnp.bfloat16)
     query_grad = query_tok.reshape(1, rows_here, HEADS * HEAD_DIM)
     return (context, query_grad, input_grad, grad_total[:, :kv_width], grad_total[:, kv_width:])
 

time: 249 us -> 246 us (0.988)
  waiting for transfers between devices: 139 us -> 128 us
  other arithmetic: 4.52 us -> 9.42 us
    psum x1 -> x0, waiting for transfers between devices: 27.7 us -> none  [body(): grad_total = lax.psum(grad_shard, 'rep').astype(jnp.bfloat16)]
    reduce_scatter x1, waiting for transfers between devices: 34.6 us -> 49.2 us  [body(): lax.psum_scatter(lax.dot_general(columns, grad_kv, (((0,), (0,)), ((), ()...]
    all_to_all x1, waiting for transfers between devices: 0.01 us -> 11.9 us  [body(): lax.all_to_all(query_back, 'seq', split_axis=0, concat_axis=1, tiled=True)]
    all_to_all x1, waiting for transfers between devices: 19.1 us -> 9.09 us  [body(): lax.all_to_all(out_part, 'seq', split_axis=0, concat_axis=1, tiled=True)]
    reduce_sum x0 -> x1, other arithmetic: none -> 2.78 us  [body(): jnp.sum(lax.all_gather(grad_shard, 'rep'), axis=0).astype(jnp.bfloat16)]
    all_gather x0 -> x1, local copies, waits for them, and re-layouts: none -> 2.56 us  [body(): lax.all_gather(grad_shard, 'rep')]
    unnamed x16 -> x14, local copies, waits for them, and re-layouts: 6.44 us -> 6.43 us
  transfers between devices with their start and end apart: 11 -> 11, of which waited for: 9 -> 9; matrix products, arithmetic and copies ran while one was open for 13% -> 14% of each run, Pallas kernels for 0% -> 0%
where the time goes in v1:
time: 246 us; the launch traced here: 245 us
  waiting for transfers between devices  128 us (52%)
  starting transfers between devices  30.8 us (13%)
  matrix products  21.8 us (9%)
  blocking collectives  21.7 us (9%)
  local copies, waits for them, and re-layouts  18.9 us (8%)
  between operations  14 us (6%)
  other arithmetic  9.42 us (4%)
    reduce_scatter x1, waiting for transfers between devices, body(): lax.psum_scatter(lax.dot_general(columns, grad_kv, (((0,), (0,)), ((), ()...  49.2 us
    all_to_all x1, waiting for transfers between devices, body(): lax.all_to_all(sent[0], 'seq', split_axis=1, concat_axis=0, tiled=True)  24.7 us
    all_gather x1, blocking collectives, body(): seg_all = lax.all_gather(segment_ids[0], 'seq', axis=0, tiled=True)  21.7 us
    all_to_all x1, waiting for transfers between devices, body(): lax.all_to_all(key_back, 'seq', split_axis=0, concat_axis=1, tiled=True)  12.3 us
    all_to_all x1, waiting for transfers between devices, body(): lax.all_to_all(query_back, 'seq', split_axis=0, concat_axis=1, tiled=True)  11.9 us
    all_gather x1, waiting for transfers between devices, body(): lax.all_gather(stacked, ('seq', 'fsdp'), axis=0, tiled=True)  9.14 us
    all_to_all x1, waiting for transfers between devices, body(): lax.all_to_all(out_part, 'seq', split_axis=0, concat_axis=1, tiled=True)  9.09 us
    unnamed x14, local copies, waits for them, and re-layouts  6.43 us
  transfers between devices with their start and end apart: 11, of which 9 were waited for; matrix products, arithmetic and copies ran while one was open for 14% of the time, Pallas kernels for 0%

profile of v1, /device:TPU:0, one launch (start us, length us, event | category | flops | bytes accessed | tf_op | source)
XLA Modules:
  0.0 244.7 jit_solution(11198750569272864409)
XLA Ops:
  7.2 1.9 pad_maximum_fusion
  9.2 2.0 copy.39
  11.2 6.3 %all-to-all-start.1 = ((bf16[128,16,128]{0,2,1:T(8,128)(2,1)}), bf16[128,16,128]{0,2,1:T(8,128)(2,1)S(1)}, u32[]{:S(2)}, u32[]{:S(2)}) async-start(bf16[128,16,128]{0,2,1:T(8,128)(2,1)} %bitcast.9), calls=%async_computation.1 | async-start | bytes 1048576 | tf_op jit(solution)/shard_map/all_to_all | solution.py:177
  17.5 2.0 copy.46
  19.6 24.7 %all-to-all-done.1 = bf16[128,16,128]{0,2,1:T(8,128)(2,1)S(1)} async-done(((bf16[128,16,128]{0,2,1:T(8,128)(2,1)}), bf16[128,16,128]{0,2,1:T(8,128)(2,1)S(1)}, u32[]{:S(2)}, u32[]{:S(2)}) %all-to-all-start.1) | async-done | bytes 524320 | tf_op jit(solution)/shard_map/all_to_all | solution.py:177
  44.2 3.6 %all-to-all-start.4 = ((bf16[128,16,128]{0,2,1:T(8,128)(2,1)}), bf16[128,16,128]{0,2,1:T(8,128)(2,1)S(1)}, u32[]{:S(2)}, u32[]{:S(2)}) async-start(bf16[128,16,128]{0,2,1:T(8,128)(2,1)} %bitcast.22), calls=%async_computation.4 | async-start | bytes 1048576 | tf_op jit(solution)/shard_map/all_to_all | solution.py:189
  47.9 21.7 %all-gather = s32[1,512]{1,0:T(1,128)S(1)} all-gather(s32[1,128]{1,0:T(1,128)S(1)} %copy-done.3), channel_id=2, replica_groups=mesh['groups'=2,'seq'=4,'rep'=2,'fsdp'=2] {'seq'}, dimensions={1}, use_global_device_ids=true | all-gather | bytes 2560 | tf_op jit(solution)/shard_map/all_gather | solution.py:184
  69.5 9.1 %all-gather.5.cloned.1.call-done = bf16[2048,1024]{1,0:T(8,128)(2,1)} async-done(((bf16[256,1024]{1,0:T(8,128)(2,1)}), bf16[2048,1024]{1,0:T(8,128)(2,1)}) %all-gather.5.cloned.1.call-update) | async-done | bytes 4194320 | tf_op jit(solution)/shard_map/all_gather | solution.py:163
  78.7 3.5 %fusion.11 = bf16[128,1024]{0,1:T(8,128)(2,1)S(1)} fusion(bf16[2048,1024]{1,0:T(8,128)(2,1)} %all-gather.5.cloned.1.call-done, bf16[1,128,2048]{2,1,0:T(8,128)(2,1)S(1)} %copy-done), kind=kOutput, calls=%fused_computation.22 | convolution fusion | flops 537001984 | bytes 4980736 | tf_op jit(solution)/shard_map/dot_general | solution.py:161
  82.2 0.8 copy.38
  83.0 3.3 %all-to-all-start = ((bf16[128,4,128]{2,0,1:T(8,128)(2,1)}), bf16[128,4,128]{2,0,1:T(8,128)(2,1)S(1)}, u32[]{:S(2)}, u32[]{:S(2)}) async-start(bf16[128,4,128]{2,0,1:T(8,128)(2,1)} %copy.38), calls=%async_computation | async-start | bytes 262144 | tf_op jit(solution)/shard_map/all_to_all | solution.py:178
  86.8 0.3 copy.48
  87.1 0.8 copy.42
  87.9 4.8 %all-to-all-done = bf16[128,4,128]{2,0,1:T(8,128)(2,1)S(1)} async-done(((bf16[128,4,128]{2,0,1:T(8,128)(2,1)}), bf16[128,4,128]{2,0,1:T(8,128)(2,1)S(1)}, u32[]{:S(2)}, u32[]{:S(2)}) %all-to-all-start) | async-done | bytes 131104 | tf_op jit(solution)/shard_map/all_to_all | solution.py:178
  92.7 3.3 %all-to-all-start.2 = ((bf16[128,4,128]{2,0,1:T(8,128)(2,1)}), bf16[128,4,128]{2,0,1:T(8,128)(2,1)S(1)}, u32[]{:S(2)}, u32[]{:S(2)}) async-start(bf16[128,4,128]{2,0,1:T(8,128)(2,1)} %copy.42), calls=%async_computation.2 | async-start | bytes 262144 | tf_op jit(solution)/shard_map/all_to_all | solution.py:179
  96.0 0.9 fusion.3
  96.9 1.0 select_reduce_fusion
  98.0 0.9 fusion.10
  99.0 1.2 copy.54
  100.2 1.8 all-to-all-done.2
  101.9 3.5 %all-to-all-start.7 = ((bf16[512,4,128]{2,1,0:T(4,128)(2,1)}), bf16[512,4,128]{2,1,0:T(4,128)(2,1)S(1)}, u32[]{:S(2)}, u32[]{:S(2)}) async-start(bf16[512,4,128]{2,1,0:T(4,128)(2,1)} %copy.54), calls=%async_computation.7 | async-start | bytes 1048576 | tf_op jit(solution)/shard_map/all_to_all | solution.py:202
  105.4 3.9 %fusion.12 = (f32[4,512]{1,0:T(4,128)S(1)}, bf16[4,512,128]{2,1,0:T(8,128)(2,1)S(1)}) fusion(bf16[4,128,4,128]{3,1,0,2:T(8,128)(2,1)S(1)} %copy.48, bf16[512,128]{1,0:T(8,128)(2,1)S(1)} %bitcast.113, f32[4,512,512]{2,1,0:T(8,128)} %copy-done.1, f32[4,512]{1,0:T(4,128)S(1)} %log_add_fusion, pred[512,512]{0,1:T(8,128)(4,1)S(1)} %fusion.13), kind=kOutput, calls=%fused_computation.24 | convolution fusion | flops 273938432 | bytes 5652480 | tf_op jit(solution)/shard_map/while/body/eval_jaxpr/while/body/hqk,khd->qhd/dot_general | solution.py:74
  109.3 1.4 fusion
  110.8 0.7 fusion.8
  111.5 0.6 copy-done.4
  112.1 1.2 copy.52
  113.3 5.2 %all-to-all-done.7 = bf16[512,4,128]{2,1,0:T(4,128)(2,1)S(1)} async-done(((bf16[512,4,128]{2,1,0:T(4,128)(2,1)}), bf16[512,4,128]{2,1,0:T(4,128)(2,1)S(1)}, u32[]{:S(2)}, u32[]{:S(2)}) %all-to-all-start.7) | async-done | bytes 524320 | tf_op jit(solution)/shard_map/all_to_all | solution.py:202
  118.5 3.5 %all-to-all-start.6 = ((bf16[512,4,128]{2,1,0:T(4,128)(2,1)}), bf16[512,4,128]{2,1,0:T(4,128)(2,1)S(1)}, u32[]{:S(2)}, u32[]{:S(2)}) async-start(bf16[512,4,128]{2,1,0:T(4,128)(2,1)} %copy.52), calls=%async_computation.6 | async-start | bytes 1048576 | tf_op jit(solution)/shard_map/all_to_all | solution.py:201
  122.2 0.7 reduce_sum.57
  123.0 12.3 %all-to-all-done.6 = bf16[512,4,128]{2,1,0:T(4,128)(2,1)S(1)} async-done(((bf16[512,4,128]{2,1,0:T(4,128)(2,1)}), bf16[512,4,128]{2,1,0:T(4,128)(2,1)S(1)}, u32[]{:S(2)}, u32[]{:S(2)}) %all-to-all-start.6) | async-done | bytes 524320 | tf_op jit(solution)/shard_map/all_to_all | solution.py:201
  135.3 0.7 reduce_sum.54
  136.1 3.2 %convert_bitcast_fusion = bf16[2048,1024]{0,1:T(8,128)(2,1)} fusion(bf16[1,128,2048]{2,1,0:T(8,128)(2,1)S(1)} %copy-done, bf16[128,512]{0,1:T(8,128)(2,1)S(1)} %bitcast.100, bf16[128,512]{0,1:T(8,128)(2,1)S(1)} %bitcast.102), kind=kOutput, calls=%fused_computation.6 | convolution fusion | flops 539492352 | bytes 4980736 | tf_op jit(solution)/shard_map/dot_general | solution.py:226
  139.4 49.2 %reduce-scatter.2.cloned.1.call-done = bf16[256,1024]{0,1:T(8,128)(2,1)} async-done(((bf16[2048,1024]{0,1:T(8,128)(2,1)}), bf16[256,1024]{0,1:T(8,128)(2,1)}) %reduce-scatter.2.cloned.1.call-update) | async-done | bytes 524304 | tf_op jit(solution)/shard_map/reduce_scatter | solution.py:225
  188.6 2.1 all_gather.21
  190.7 1.2 copy.44
  191.9 3.5 %all-to-all-start.3 = ((bf16[512,4,128]{2,1,0:T(4,128)(2,1)}), bf16[512,4,128]{2,1,0:T(4,128)(2,1)S(1)}, u32[]{:S(2)}, u32[]{:S(2)}) async-start(bf16[512,4,128]{2,1,0:T(4,128)(2,1)} %copy.44), calls=%async_computation.3 | async-start | bytes 1048576 | tf_op jit(solution)/shard_map/all_to_all | solution.py:186
  195.4 2.7 %fusion.9 = bf16[512,4,128]{2,0,1:T(8,128)(2,1)S(1)} fusion(bf16[4,512,512]{1,2,0:T(8,128)(2,1)} %copy-done.4, bf16[512,128]{1,0:T(8,128)(2,1)S(1)} %bitcast.105), kind=kOutput, calls=%fused_computation.19 | convolution fusion | flops 268959744 | bytes 2752512 | tf_op jit(solution)/shard_map/while/body/eval_jaxpr/while/body/hqk,khd->qhd/dot_general | solution.py:126
  198.2 1.2 copy.50
  199.4 9.1 %all-to-all-done.3 = bf16[512,4,128]{2,1,0:T(4,128)(2,1)S(1)} async-done(((bf16[512,4,128]{2,1,0:T(4,128)(2,1)}), bf16[512,4,128]{2,1,0:T(4,128)(2,1)S(1)}, u32[]{:S(2)}, u32[]{:S(2)}) %all-to-all-start.3) | async-done | bytes 524320 | tf_op jit(solution)/shard_map/all_to_all | solution.py:186
  208.5 3.5 %all-to-all-start.5 = ((bf16[512,4,128]{2,1,0:T(4,128)(2,1)}), bf16[512,4,128]{2,1,0:T(4,128)(2,1)S(1)}, u32[]{:S(2)}, u32[]{:S(2)}) async-start(bf16[512,4,128]{2,1,0:T(4,128)(2,1)} %copy.50), calls=%async_computation.5 | async-start | bytes 1048576 | tf_op jit(solution)/shard_map/all_to_all | solution.py:200
  212.2 1.2 reshape.232
  213.3 11.9 %all-to-all-done.5 = bf16[512,4,128]{2,1,0:T(4,128)(2,1)S(1)} async-done(((bf16[512,4,128]{2,1,0:T(4,128)(2,1)}), bf16[512,4,128]{2,1,0:T(4,128)(2,1)S(1)}, u32[]{:S(2)}, u32[]{:S(2)}) %all-to-all-start.5) | async-done | bytes 524320 | tf_op jit(solution)/shard_map/all_to_all | solution.py:200
  225.4 1.2 reshape.233
  226.6 4.5 %fusion.5 = bf16[1,128,2048]{2,1,0:T(8,128)(2,1)} fusion(bf16[2048,1024]{1,0:T(8,128)(2,1)} %all-gather.5.cloned.1.call-done, bf16[128,512]{0,1:T(8,128)(2,1)S(1)} %bitcast.101, bf16[128,512]{0,1:T(8,128)(2,1)S(1)} %bitcast.103), kind=kOutput, calls=%fused_computation.11 | convolution fusion | flops 537657344 | bytes 4980736 | tf_op jit(solution)/shard_map/dot_general | solution.py:217
  231.1 2.6 %reshape.239 = f32[2,256,1024]{1,0,2:T(2,128)S(1)} reshape(f32[512,1024]{0,1:T(8,128)} %all-gather.7.cloned.1.call-done) | data formatting | bytes 4194304 | tf_op jit(solution)/shard_map/all_gather | solution.py:233
  233.6 2.8 %reduce_sum.60 = bf16[256,1024]{0,1:T(8,128)(2,1)S(1)} reduce(f32[2,256,1024]{1,0,2:T(2,128)S(1)} %reshape.239, f32[]{:T(128)} %constant.105.clone.1), dimensions={0}, to_apply=%region_5.6 | reduce | flops 262144 | bytes 2621444 | tf_op jit(solution)/shard_map/reduce_sum | solution.py:233
  236.5 0.8 copy.57
  237.3 0.8 copy.56
  (27 shorter events, 1.6 us)
Async XLA Ops:
  7.2 71.5 %copy-start = (bf16[1,128,2048]{2,1,0:T(8,128)(2,1)S(1)}, bf16[1,128,2048]{2,1,0:T(8,128)(2,1)}, u32[]{:S(2)}) copy-start(bf16[1,128,2048]{2,1,0:T(8,128)(2,1)} %param.6) | copy-start | bytes 1572868
  7.2 40.7 %copy-start.3 = (s32[1,128]{1,0:T(1,128)S(1)}, s32[1,128]{1,0:T(1,128)}, u32[]{:S(2)}) copy-start(s32[1,128]{1,0:T(1,128)} %param.10) | copy-start | bytes 1540
  7.2 71.5 %all-gather.5.cloned.1.call-start = ((), (), s32[]{:S(2)}) async-start(), calls=%async_computation.9 | async-start | bytes 4718592 | tf_op jit(solution)/shard_map/all_gather | solution.py:163
  11.2 33.0 %all-to-all-start.1 = ((bf16[128,16,128]{0,2,1:T(8,128)(2,1)}), bf16[128,16,128]{0,2,1:T(8,128)(2,1)S(1)}, u32[]{:S(2)}, u32[]{:S(2)}) async-start(bf16[128,16,128]{0,2,1:T(8,128)(2,1)} %bitcast.9), calls=%async_computation.1 | async-start | bytes 1048576 | tf_op jit(solution)/shard_map/all_to_all | solution.py:177
  44.2 38.7 %all-to-all-start.4 = ((bf16[128,16,128]{0,2,1:T(8,128)(2,1)}), bf16[128,16,128]{0,2,1:T(8,128)(2,1)S(1)}, u32[]{:S(2)}, u32[]{:S(2)}) async-start(bf16[128,16,128]{0,2,1:T(8,128)(2,1)} %bitcast.22), calls=%async_computation.4 | async-start | bytes 1048576 | tf_op jit(solution)/shard_map/all_to_all | solution.py:189
  83.0 9.7 %all-to-all-start = ((bf16[128,4,128]{2,0,1:T(8,128)(2,1)}), bf16[128,4,128]{2,0,1:T(8,128)(2,1)S(1)}, u32[]{:S(2)}, u32[]{:S(2)}) async-start(bf16[128,4,128]{2,0,1:T(8,128)(2,1)} %copy.38), calls=%async_computation | async-start | bytes 262144 | tf_op jit(solution)/shard_map/all_to_all | solution.py:178
  92.7 9.2 %all-to-all-start.2 = ((bf16[128,4,128]{2,0,1:T(8,128)(2,1)}), bf16[128,4,128]{2,0,1:T(8,128)(2,1)S(1)}, u32[]{:S(2)}, u32[]{:S(2)}) async-start(bf16[128,4,128]{2,0,1:T(8,128)(2,1)} %copy.42), calls=%async_computation.2 | async-start | bytes 262144 | tf_op jit(solution)/shard_map/all_to_all | solution.py:179
  96.9 2.0 copy-start.1
  101.9 16.6 %all-to-all-start.7 = ((bf16[512,4,128]{2,1,0:T(4,128)(2,1)}), bf16[512,4,128]{2,1,0:T(4,128)(2,1)S(1)}, u32[]{:S(2)}, u32[]{:S(2)}) async-start(bf16[512,4,128]{2,1,0:T(4,128)(2,1)} %copy.54), calls=%async_computation.7 | async-start | bytes 1048576 | tf_op jit(solution)/shard_map/all_to_all | solution.py:202
  105.4 3.9 %copy-start.2 = (f32[4,512,512]{2,1,0:T(8,128)S(1)}, f32[4,512,512]{2,1,0:T(8,128)}, u32[]{:S(2)}) copy-start(f32[4,512,512]{2,1,0:T(8,128)} %copy-done.1) | copy-start | bytes 12582916
  110.7 1.4 copy-start.4
  118.5 16.8 %all-to-all-start.6 = ((bf16[512,4,128]{2,1,0:T(4,128)(2,1)}), bf16[512,4,128]{2,1,0:T(4,128)(2,1)S(1)}, u32[]{:S(2)}, u32[]{:S(2)}) async-start(bf16[512,4,128]{2,1,0:T(4,128)(2,1)} %copy.52), calls=%async_computation.6 | async-start | bytes 1048576 | tf_op jit(solution)/shard_map/all_to_all | solution.py:201
  122.0 66.6 %reduce-scatter.2.cloned.1.call-start = ((), (), s32[]{:S(2)}) async-start(), calls=%async_computation.10 | async-start | bytes 4718592 | tf_op jit(solution)/shard_map/reduce_scatter | solution.py:225
  139.4 91.7 %all-gather.7.cloned.1.call-start = ((), (), s32[]{:S(2)}) async-start(), calls=%async_computation.11 | async-start | bytes 3145728 | tf_op jit(solution)/shard_map/all_gather | solution.py:233
  191.9 16.5 %all-to-all-start.3 = ((bf16[512,4,128]{2,1,0:T(4,128)(2,1)}), bf16[512,4,128]{2,1,0:T(4,128)(2,1)S(1)}, u32[]{:S(2)}, u32[]{:S(2)}) async-start(bf16[512,4,128]{2,1,0:T(4,128)(2,1)} %copy.44), calls=%async_computation.3 | async-start | bytes 1048576 | tf_op jit(solution)/shard_map/all_to_all | solution.py:186
  208.5 16.7 %all-to-all-start.5 = ((bf16[512,4,128]{2,1,0:T(4,128)(2,1)}), bf16[512,4,128]{2,1,0:T(4,128)(2,1)S(1)}, u32[]{:S(2)}, u32[]{:S(2)}) async-start(bf16[512,4,128]{2,1,0:T(4,128)(2,1)} %copy.50), calls=%async_computation.5 | async-start | bytes 1048576 | tf_op jit(solution)/shard_map/all_to_all | solution.py:200
Sparse Core Ops, SparseCore 0:
  10.2 68.4 all-gather.4
  139.5 49.0 reduce-scatter.1
  190.9 31.2 all-gather.6
